TPU v7x, 32 devices: a whole 2x2x4 slice. The times are simulated.
32 devices in a mesh: dp: 4 (over x, core), seq: 8 (over z, y).
Axes of the slice: x: 2, y: 2, z: 4, core: 2. Of those that a mesh axis runs over, the one named last changes fastest.
Arguments:
- tokens: bfloat16 [32768, 1152], P(('dp', 'seq')), may hold values from -6 to 6
- condition: bfloat16 [128, 1152], P('dp'), may hold values from -6 to 6
- lengths: int32 [128], P(('dp', 'seq')), may hold values from 1 to 256, 22937 in all
- kept_index: int32 [128, 256], P(('dp', 'seq')), may hold values from 0 to 255, each once within a row
- heads_weight: bfloat16 [1152, 3456], P('seq'), may hold values from -0.1875 to 0.1875
- heads_bias: bfloat16 [2304], replicated, may hold values from -1.5 to 1.5
- merge_weight: bfloat16 [1152, 1152], P('seq'), may hold values from -1.5 to 1.5
- merge_bias: bfloat16 [1152], replicated, may hold values from -4 to 4
- up_weight: bfloat16 [1152, 4608], P('seq'), may hold values from -0.1875 to 0.1875
- up_bias: bfloat16 [4608], replicated, may hold values from -4 to 4
- down_weight: bfloat16 [1152, 4608], P('seq'), may hold values from -0.1875 to 0.1875
- down_bias: bfloat16 [1152], replicated, may hold values from -4 to 4
- modulate_weight: bfloat16 [1152, 6912], P('seq'), may hold values from -0.1875 to 0.1875
- modulate_bias: bfloat16 [6912], replicated, may hold values from -4 to 4
- relative_table: bfloat16 [16, 961], replicated, may hold values from -6 to 6
- cotangent: bfloat16 [32768, 1152], P(('dp', 'seq')), may hold values from -6 to 6
Outputs:
- output: bfloat16 [32768, 1152], P(('dp', 'seq'))
- tokens_grad: float32 [32768, 1152], P(('dp', 'seq'))
- heads_weight_grad: float32 [1152, 3456], P('seq')
- merge_weight_grad: float32 [1152, 1152], P('seq')
- up_weight_grad: float32 [1152, 4608], P('seq')
- down_weight_grad: float32 [1152, 4608], P('seq')
- modulate_weight_grad: float32 [1152, 6912], P('seq')
- heads_bias_grad: float32 [2304], replicated
- merge_bias_grad: float32 [1152], replicated
- up_bias_grad: float32 [4608], replicated
- down_bias_grad: float32 [1152], replicated
- modulate_bias_grad: float32 [6912], replicated
- relative_table_grad: float32 [16, 961], replicated
Inputs may be any that keep to these rules, and one draw needn't show every extreme that they name: The first lengths[s] slots of sample s hold its kept tokens, the rest are empty. Each sample's row is a permutation of the 256 patch positions; slot r's patch lies at row kept_index // 16, column kept_index % 16.
All inputs are finite; a program needn't handle non-finite values. No bound on the sum of `lengths` on one device may be relied on, other than what follows from the above.
Results may differ from a plain program's by a relative error of at most 0.019.
Values may be sent and summed in bfloat16 or wider, within the bound.
No kernel may reach another device: no remote copies, remote signals or barrier semaphores. Data moves between devices by JAX's collectives and lax.ppermute only.
A program may use at most 320 MiB of HBM per device.

v0:
```python
from functools import partial
import math
import jax
import jax.numpy as jnp
from jax import lax
from jax.sharding import PartitionSpec as P

D = 1152
HEADS = 16
HEAD = 72
FF = 4608
SIDE = 16
MICRO = 2
SAMP_DEV = 4
GRID = 256
epsilon = 1e-06


def layer_norm(values):
    center = values - jnp.mean(values, axis=-1, keepdims=True)
    spread = jnp.mean(center * center, axis=-1, keepdims=True)
    return center * lax.rsqrt(spread + epsilon)


def modulated(values, scales, shifts):
    return layer_norm(values) * (1.0 + scales) + shifts


def gelu_tanh(values):
    return jax.nn.gelu(values, approximate=True)


def fold_rows(left, portion):
    return jnp.dot(left, portion, preferred_element_type=jnp.float32)


def right_transposed(left, portion):
    return lax.dot_general(
        left, portion, (((1,), (1,)), ((), ())), preferred_element_type=jnp.float32
    )


def column_outer(left, right):
    return lax.dot_general(
        left, right, (((0,), (0,)), ((), ())), preferred_element_type=jnp.float32
    )


def relative_index(positions):
    row_place = positions // SIDE
    col_place = positions % SIDE
    row_gap = row_place[..., :, None] - row_place[..., None, :] + (SIDE - 1)
    col_gap = col_place[..., :, None] - col_place[..., None, :] + (SIDE - 1)
    return row_gap * (2 * SIDE - 1) + col_gap


def slot_onehot(index_pair):
    return (index_pair[..., :, None] == jnp.arange(GRID)[None, None, :]).astype(jnp.bfloat16)


def pair_scores(packed, lens_pair, index_pair, position_bias):
    parts = packed.reshape(2, GRID, 3, HEADS, HEAD)
    queries = parts[:, :, 0]
    key_part = parts[:, :, 1]
    value_part = parts[:, :, 2]
    scaling = 1.0 / math.sqrt(HEAD)
    onehot = slot_onehot(index_pair)
    rows_placed = jnp.einsum(
        "srp,hpq->hsrq", onehot, position_bias, preferred_element_type=jnp.float32
    ).astype(jnp.bfloat16)
    bias_pair = jnp.einsum(
        "hsrq,skq->hsrk", rows_placed, onehot, preferred_element_type=jnp.float32
    )
    scores = (
        jnp.einsum("sqhe,skhe->hsqk", queries, key_part, preferred_element_type=jnp.float32)
        * scaling
    )
    scores = scores + bias_pair
    living = jnp.arange(GRID)[None, :] < lens_pair[:, None]
    scores = jnp.where(living[None, :, None, :], scores, -1e30)
    return (scores, queries, key_part, value_part, onehot)


def attend_pair(arguments, position_bias):
    packed, lens_pair, index_pair = arguments
    scores, queries, key_part, value_part, onehot = pair_scores(
        packed, lens_pair, index_pair, position_bias
    )
    peak = jnp.max(scores, axis=-1, keepdims=True)
    expo = jnp.exp(scores - peak)
    mass = jnp.sum(expo, axis=-1, keepdims=True)
    probs_low = (expo / mass).astype(jnp.bfloat16)
    mixed = jnp.einsum("hsqk,skhe->sqhe", probs_low, value_part, preferred_element_type=jnp.float32)
    return (mixed.astype(jnp.bfloat16).reshape(2 * GRID, D), (peak + jnp.log(mass))[..., 0])


def attend_pair_back(arguments, position_bias):
    packed, lens_pair, index_pair, logsum, grad_mixed = arguments
    scores, queries, key_part, value_part, onehot = pair_scores(
        packed, lens_pair, index_pair, position_bias
    )
    probs = jnp.exp(scores - logsum[..., None])
    grad_mixed = grad_mixed.reshape(2, GRID, HEADS, HEAD)
    grad_probs = jnp.einsum(
        "sqhe,skhe->hsqk", grad_mixed, value_part, preferred_element_type=jnp.float32
    )
    inner = jnp.sum(probs * grad_probs, axis=-1, keepdims=True)
    grad_scores = (probs * (grad_probs - inner)).astype(jnp.bfloat16)
    scaling = 1.0 / math.sqrt(HEAD)
    grad_query = (
        jnp.einsum("hsqk,skhe->sqhe", grad_scores, key_part, preferred_element_type=jnp.float32)
        * scaling
    )
    grad_key = (
        jnp.einsum("hsqk,sqhe->skhe", grad_scores, queries, preferred_element_type=jnp.float32)
        * scaling
    )
    grad_value = jnp.einsum(
        "hsqk,sqhe->skhe",
        probs.astype(jnp.bfloat16),
        grad_mixed,
        preferred_element_type=jnp.float32,
    )
    stacked = (
        jnp.stack([grad_query, grad_key, grad_value], axis=2)
        .astype(jnp.bfloat16)
        .reshape(2 * GRID, 3 * D)
    )
    rows_back = jnp.einsum(
        "hsrk,srp->hspk", grad_scores, onehot, preferred_element_type=jnp.float32
    ).astype(jnp.bfloat16)
    placed_grad = jnp.einsum("hspk,skq->hpq", rows_back, onehot, preferred_element_type=jnp.float32)
    return (stacked, placed_grad)


def offsets_table(placed_grad):
    spots = jnp.arange(SIDE)
    reach = jnp.arange(2 * SIDE - 1)
    gaps = (
        spots[:, None, None] - spots[None, :, None] + (SIDE - 1) == reach[None, None, :]
    ).astype(jnp.float32)
    grid_grad = placed_grad.reshape(HEADS, SIDE, SIDE, SIDE, SIDE)
    by_rows = jnp.einsum("hwxyz,wya->haxz", grid_grad, gaps, precision=lax.Precision.HIGHEST)
    return jnp.einsum("haxz,xzb->hab", by_rows, gaps, precision=lax.Precision.HIGHEST).reshape(
        HEADS, (2 * SIDE - 1) ** 2
    )


def local(
    tokens,
    condition,
    lengths,
    kept_index,
    heads_weight,
    heads_bias,
    merge_weight,
    merge_bias,
    up_weight,
    up_bias,
    down_weight,
    down_bias,
    modulate_weight,
    modulate_bias,
    relative_table,
    cotangent,
):
    position = lax.axis_index("seq")
    position_bias = jnp.take(relative_table, relative_index(jnp.arange(GRID)), axis=1)
    own_cond = lax.dynamic_slice_in_dim(condition, position * SAMP_DEV, SAMP_DEV, 0)
    own_silu = jax.nn.silu(own_cond.astype(jnp.float32)).astype(jnp.bfloat16)
    modulation = fold_rows(own_silu, lax.all_gather(modulate_weight, "seq", axis=0, tiled=True))
    modulation = (modulation + modulate_bias.astype(jnp.float32)).reshape(SAMP_DEV, 1, 6, D)
    full_bias = jnp.concatenate(
        [heads_bias[:D], jnp.zeros((D,), jnp.bfloat16), heads_bias[D:]]
    ).astype(jnp.float32)
    parts_count = MICRO
    samples = SAMP_DEV // parts_count
    rows = samples * GRID
    pairs = samples // 2
    kept = {
        "out": [],
        "tgrad": [],
        "mgrad": [],
        "hone": [],
        "gpack": [],
        "attn": [],
        "gbranch": [],
        "htwo": [],
        "gup": [],
        "gmlp": [],
        "act": [],
    }
    placed_total = jnp.zeros((HEADS, GRID, GRID), jnp.float32)
    for part in range(parts_count):
        slab = tokens[part * rows : (part + 1) * rows].astype(jnp.float32).reshape(samples, GRID, D)
        mods = modulation[part * samples : (part + 1) * samples]
        shift_one, scale_one, gate_one, shift_two, scale_two, gate_two = [
            mods[:, :, index] for index in range(6)
        ]
        lens_part = lengths[part * samples : (part + 1) * samples]
        index_part = kept_index[part * samples : (part + 1) * samples]
        living = (jnp.arange(GRID)[None, :] < lens_part[:, None])[:, :, None]
        hidden_one = modulated(slab, scale_one, shift_one).astype(jnp.bfloat16).reshape(rows, D)
        packed = (
            fold_rows(hidden_one, lax.all_gather(heads_weight, "seq", axis=0, tiled=True))
            + full_bias
        ).astype(jnp.bfloat16)
        packed_pairs = packed.reshape(pairs, 2 * GRID, 3 * D)
        lens_pairs = lens_part.reshape(pairs, 2)
        index_pairs = index_part.reshape(pairs, 2, GRID)
        attended, logsum = lax.map(
            partial(attend_pair, position_bias=position_bias),
            (packed_pairs, lens_pairs, index_pairs),
        )
        attended = attended.reshape(rows, D)
        branch = fold_rows(
            attended, lax.all_gather(merge_weight, "seq", axis=0, tiled=True)
        ) + merge_bias.astype(jnp.float32)
        branch = branch.reshape(samples, GRID, D)
        middle = slab + gate_one * branch
        hidden_two = modulated(middle, scale_two, shift_two).astype(jnp.bfloat16).reshape(rows, D)
        up_value = fold_rows(
            hidden_two, lax.all_gather(up_weight, "seq", axis=0, tiled=True)
        ) + up_bias.astype(jnp.float32)
        activated = gelu_tanh(up_value).astype(jnp.bfloat16)
        mlp_out = right_transposed(
            activated, lax.all_gather(down_weight, "seq", axis=0, tiled=True)
        )
        mlp_out = (mlp_out + down_bias.astype(jnp.float32)).reshape(samples, GRID, D)
        final = jnp.where(living, middle + gate_two * mlp_out, 0.0)
        kept["out"].append(final.astype(jnp.bfloat16).reshape(rows, D))
        grad_final = jnp.where(
            living,
            cotangent[part * rows : (part + 1) * rows]
            .astype(jnp.float32)
            .reshape(samples, GRID, D),
            0.0,
        )
        gate_two_grad = jnp.sum(grad_final * mlp_out, axis=1, keepdims=True)
        grad_mlp = (gate_two * grad_final).astype(jnp.bfloat16).reshape(rows, D)
        grad_act = fold_rows(grad_mlp, lax.all_gather(down_weight, "seq", axis=0, tiled=True))
        grad_up = jax.vjp(gelu_tanh, up_value)[1](grad_act)[0].astype(jnp.bfloat16)
        grad_hidden_two = right_transposed(
            grad_up, lax.all_gather(up_weight, "seq", axis=0, tiled=True)
        )
        middle_ln, scale_two_grad, shift_two_grad = jax.vjp(
            modulated, middle, scale_two, shift_two
        )[1](grad_hidden_two.reshape(samples, GRID, D))
        grad_middle = grad_final + middle_ln
        gate_one_grad = jnp.sum(grad_middle * branch, axis=1, keepdims=True)
        grad_branch = (gate_one * grad_middle).astype(jnp.bfloat16).reshape(rows, D)
        grad_attended = right_transposed(
            grad_branch, lax.all_gather(merge_weight, "seq", axis=0, tiled=True)
        ).astype(jnp.bfloat16)
        grad_packed, placed_parts = lax.map(
            partial(attend_pair_back, position_bias=position_bias),
            (
                packed_pairs,
                lens_pairs,
                index_pairs,
                logsum,
                grad_attended.reshape(pairs, 2 * GRID, D),
            ),
        )
        grad_packed = grad_packed.reshape(rows, 3 * D)
        placed_total = placed_total + jnp.sum(placed_parts, axis=0)
        grad_hidden_one = right_transposed(
            grad_packed, lax.all_gather(heads_weight, "seq", axis=0, tiled=True)
        )
        slab_ln, scale_one_grad, shift_one_grad = jax.vjp(modulated, slab, scale_one, shift_one)[1](
            grad_hidden_one.reshape(samples, GRID, D)
        )
        kept["tgrad"].append((grad_middle + slab_ln).reshape(rows, D))
        kept["mgrad"].append(
            jnp.concatenate(
                [
                    shift_one_grad,
                    scale_one_grad,
                    gate_one_grad,
                    shift_two_grad,
                    scale_two_grad,
                    gate_two_grad,
                ],
                axis=-1,
            ).reshape(samples, 6 * D)
        )
        kept["hone"].append(hidden_one)
        kept["gpack"].append(grad_packed)
        kept["attn"].append(attended)
        kept["gbranch"].append(grad_branch)
        kept["htwo"].append(hidden_two)
        kept["gup"].append(grad_up)
        kept["gmlp"].append(grad_mlp)
        kept["act"].append(activated)
    table_grad = offsets_table(placed_total)
    joined = {name: jnp.concatenate(items, axis=0) for name, items in kept.items()}
    mod_grad = joined["mgrad"].astype(jnp.bfloat16)
    pieces = [
        column_outer(joined["hone"], joined["gpack"]),
        column_outer(joined["attn"], joined["gbranch"]),
        column_outer(joined["htwo"], joined["gup"]),
        column_outer(joined["gmlp"], joined["act"]),
        column_outer(own_silu, mod_grad),
    ]
    summed = lax.psum_scatter(
        jnp.concatenate(pieces, axis=1).astype(jnp.bfloat16), "seq", scatter_dimension=0, tiled=True
    )
    share = lax.psum_scatter(summed, "dp", scatter_dimension=0, tiled=True).astype(jnp.float32)
    replicated = lax.all_gather(share.astype(jnp.bfloat16), "dp", axis=0, tiled=True).astype(
        share.dtype
    )
    packed_sums = jnp.sum(joined["gpack"], axis=0, dtype=jnp.float32)
    heads_part = jnp.concatenate([packed_sums[:D], packed_sums[2 * D :]])
    merge_part = jnp.sum(joined["gbranch"], axis=0, dtype=jnp.float32)
    up_part = jnp.sum(joined["gup"], axis=0, dtype=jnp.float32)
    down_part = jnp.sum(joined["gmlp"], axis=0, dtype=jnp.float32)
    modulate_part = jnp.sum(mod_grad, axis=0, dtype=jnp.float32)
    heads_total, merge_total, up_total, down_total, modulate_total, table_total = lax.psum(
        (heads_part, merge_part, up_part, down_part, modulate_part, table_grad), ("dp", "seq")
    )
    edges = [0, 3 * D, 4 * D, 4 * D + FF, 4 * D + 2 * FF, 10 * D + 2 * FF]
    return (
        joined["out"],
        joined["tgrad"],
        replicated[:, edges[0] : edges[1]],
        replicated[:, edges[1] : edges[2]],
        replicated[:, edges[2] : edges[3]],
        replicated[:, edges[3] : edges[4]],
        replicated[:, edges[4] : edges[5]],
        heads_total,
        merge_total,
        up_total,
        down_total,
        modulate_total,
        table_total,
    )


def solution(mesh):
    in_specs = (
        P(("dp", "seq"), None),
        P("dp", None),
        P(("dp", "seq")),
        P(("dp", "seq"), None),
        P("seq", None),
        P(),
        P("seq", None),
        P(),
        P("seq", None),
        P(),
        P("seq", None),
        P(),
        P("seq", None),
        P(),
        P(),
        P(("dp", "seq"), None),
    )
    out_specs = (
        P(("dp", "seq"), None),
        P(("dp", "seq"), None),
        P("seq", None),
        P("seq", None),
        P("seq", None),
        P("seq", None),
        P("seq", None),
        P(),
        P(),
        P(),
        P(),
        P(),
        P(),
    )
    return jax.shard_map(local, mesh=mesh, in_specs=in_specs, out_specs=out_specs, check_vma=False)
```

profile of v0, /device:TPU:8, one launch (start us, length us, event | category | flops | bytes accessed | tf_op | source)
XLA Modules:
  0.0 2067.6 jit_solution(3447131822799105786)
XLA Ops:
  21.8 4.3 slice_convert_fusion.1
  26.2 227.7 %gather_fusion = bf16[65536,16]{1,0:T(8,128)(2,1)} fusion(bf16[16,961]{0,1:T(8,128)(2,1)S(1)} %copy.147, s32[65536]{0:T(1024)S(1)} %broadcast_clamp_fusion), kind=kCustom, calls=%fused_computation | custom fusion | bytes 4456448 | tf_op jit(solution)/shard_map/jit(_take)/gather | solution.py:168
  253.8 16.7 copy.148
  270.6 5.1 convert_bitcast_fusion
  279.7 7.9 convolution_add_fusion
  292.3 54.5 %all-gather.10.cloned.1.call-done = bf16[1152,3456]{1,0:T(8,128)(2,1)} async-done(((bf16[144,3456]{1,0:T(8,128)(2,1)}), bf16[1152,3456]{1,0:T(8,128)(2,1)}) %all-gather.10.cloned.1.call-update) | async-done | bytes 7962640 | tf_op jit(solution)/shard_map/all_gather | solution.py:205
  346.7 9.5 add_convert_fusion.1
  356.3 5.8 copy.143
  362.1 8.3 reshape.859
  370.4 15.9 fusion.217
  399.5 4.5 all-gather.12.cloned.1.call-done
  404.0 6.8 fusion.212
  411.4 11.2 add_convert_fusion
  422.6 5.7 copy.152
  428.3 8.3 reshape.861
  467.8 87.5 %all-gather.14.cloned.1.call-done = bf16[1152,4608]{1,0:T(8,128)(2,1)} async-done(((bf16[144,4608]{1,0:T(8,128)(2,1)}), bf16[1152,4608]{1,0:T(8,128)(2,1)}) %all-gather.14.cloned.1.call-update) | async-done | bytes 10616848 | tf_op jit(solution)/shard_map/all_gather | solution.py:223
  555.3 11.7 fusion.231
  566.9 8.9 fusion.230
  575.8 132.2 %all-gather.16.cloned.1.call-done = bf16[1152,4608]{1,0:T(8,128)(2,1)} async-done(((bf16[144,4608]{1,0:T(8,128)(2,1)}), bf16[1152,4608]{1,0:T(8,128)(2,1)}) %all-gather.16.cloned.1.call-update) | async-done | bytes 10616848 | tf_op jit(solution)/shard_map/all_gather | solution.py:227
  708.0 11.6 fusion.232
  719.6 24.2 %fusion.11 = (bf16[512,4608]{1,0:T(8,128)(2,1)}, bf16[512,4608]{1,0:T(8,128)(2,1)}, bf16[512,4608]{1,0:T(8,128)(2,1)}, bf16[512,4608]{1,0:T(8,128)(2,1)}) fusion(f32[512,4608]{1,0:T(8,128)} %fusion.230, f32[4608]{0:T(1024)S(1)} %copy-done.104, f32[512,4608]{1,0:T(8,128)} %fusion.231, f32[512,4608]{1,0:T(8,128)} %fusion.232, ...), kind=kOutput, calls=%fused_computation.21 | convolution fusion | flops 5544345600 | bytes 59000832 | tf_op jit(solution)/shard_map/dot_general | solution.py:34
  743.8 12.7 multiply_reduce_fusion.11
  757.2 13.2 multiply_reduce_fusion.9
  771.0 14.4 fusion.210
  785.5 13.1 fusion.211
  810.9 5.3 multiply_reduce_fusion.1
  832.8 4.8 convolution_convert_fusion.4
  847.4 6.1 multiply_reduce_fusion
  864.9 5.5 copy.182
  874.3 5.2 copy.183
  883.6 8.8 multiply_reduce_fusion.10
  899.8 10.3 multiply_reduce_fusion.8
  910.2 4.8 multiply_reduce_fusion.4
  916.6 10.9 fusion.4
  931.0 17.3 fusion.3
  948.4 16.6 fusion.2
  975.5 8.7 fusion.1
  984.2 748.7 %reduce-scatter.4.cloned.1.call-done = bf16[144,20736]{1,0:T(8,128)(2,1)} async-done(((bf16[1152,20736]{1,0:T(8,128)(2,1)}), bf16[144,20736]{1,0:T(8,128)(2,1)}) %reduce-scatter.4.cloned.1.call-update) | async-done | bytes 5971984 | tf_op jit(solution)/shard_map/reduce_scatter | solution.py:305
  1732.9 62.0 %fusion = bf16[40,20736]{1,0:T(8,128)(2,1)} fusion(bf16[144,20736]{1,0:T(8,128)(2,1)} %reduce-scatter.4.cloned.1.call-done), kind=kCustom, calls=%all-reduce-scatter | all-reduce-scatter fusion | flops 3317761 | bytes 7631360
  1800.4 17.0 concatenate.72
  1820.6 6.8 fusion.32
  1827.4 8.1 bitcast_add_fusion.2
  1835.4 19.8 add.547
  1855.2 33.3 %fusion.185 = f32[31,16,16,16,1]{0,3,2,4,1:T(8,128)} fusion(f32[16,16,16,16,16]{4,3,2,1,0:T(8,128)} %add.547, s32[16,16]{1,0:T(8,128)S(1)} %subtract_add_fusion), kind=kOutput, calls=%fused_computation.258 | convolution fusion | flops 390078208 | bytes 4703232 | tf_op jit(solution)/shard_map/hwxyz,wya->haxz/dot_general | solution.py:143
  1911.9 4.3 convert_reduce_fusion
  1916.3 10.3 reshape.899
  1926.6 5.7 fusion.216
  1938.7 113.8 %all-reduce.5.cloned.1.call-done = (f32[2304]{0:T(1024)}, f32[1152]{0:T(1024)}, f32[4608]{0:T(1024)}, f32[1152]{0:T(1024)}, f32[6912]{0:T(1024)}, /*index=5*/f32[16,961]{1,0:T(8,128)}) async-done(((f32[2304]{0:T(1024)}, f32[1152]{0:T(1024)}, f32[4608]{0:T(1024)}, f32[1152]{0:T(1024)}, f32[6912]{0:T(1024)}, /*index=5*/f32[16,961]{1,0:T(8,128)}), (f32[2304]{0:T(1024)}, f32[1152]{0:T(1024)}, f32[4608]{0:T(1024)}, ...) | async-done | bytes 126032 | tf_op jit(solution)/shard_map/psum | solution.py:318
  (496 shorter events, 194.9 us)
Async XLA Ops:
  7.2 272.5 %all-gather.8.cloned.1.call-start = ((), (), s32[]{:S(2)}) async-start(), calls=%async_computation.1 | async-start | bytes 17915904 | tf_op jit(solution)/shard_map/all_gather | solution.py:171
  7.9 338.8 %all-gather.10.cloned.1.call-start = ((), (), s32[]{:S(2)}) async-start(), calls=%async_computation.2 | async-start | bytes 8957952 | tf_op jit(solution)/shard_map/all_gather | solution.py:205
  8.7 395.3 %all-gather.12.cloned.1.call-start = ((), (), s32[]{:S(2)}) async-start(), calls=%async_computation.3 | async-start | bytes 2985984 | tf_op jit(solution)/shard_map/all_gather | solution.py:217
  9.4 545.9 %all-gather.14.cloned.1.call-start = ((), (), s32[]{:S(2)}) async-start(), calls=%async_computation.4 | async-start | bytes 11943936 | tf_op jit(solution)/shard_map/all_gather | solution.py:223
  10.0 698.0 %all-gather.16.cloned.1.call-start = ((), (), s32[]{:S(2)}) async-start(), calls=%async_computation.5 | async-start | bytes 11943936 | tf_op jit(solution)/shard_map/all_gather | solution.py:227
  10.6 1722.4 %reduce-scatter.4.cloned.1.call-start = ((), (), s32[]{:S(2)}) async-start(), calls=%async_computation.6 | async-start | bytes 53747712 | tf_op jit(solution)/shard_map/reduce_scatter | solution.py:305
  17.2 253.4 %copy-start.135 = (s32[2,256]{1,0:T(2,128)}, s32[2,256]{1,0:T(2,128)S(1)}, u32[]{:S(2)}) copy-start(s32[2,256]{1,0:T(2,128)S(1)} %get-tuple-element.193) | copy-start | bytes 6148
  17.2 370.5 %copy-start.98 = (s32[2,256]{1,0:T(2,128)}, s32[2,256]{1,0:T(2,128)S(1)}, u32[]{:S(2)}) copy-start(s32[2,256]{1,0:T(2,128)S(1)} %get-tuple-element.192) | copy-start | bytes 6148
  292.3 64.0 %copy-start.63 = (bf16[512,1152]{1,0:T(8,128)(2,1)}, bf16[512,1152]{1,0:T(8,128)(2,1)S(1)}, u32[]{:S(2)}) copy-start(bf16[512,1152]{1,0:T(8,128)(2,1)S(1)} %fusion.98) | copy-start | bytes 3538948
  398.8 12.0 copy-start.54
  399.5 11.3 copy-start.70
  461.2 309.8 %copy-start.74 = (f32[2,1152]{1,0:T(2,128)}, f32[2,1152]{1,0:T(2,128)S(1)}, u32[]{:S(2)}) copy-start(f32[2,1152]{1,0:T(2,128)S(1)} %get-tuple-element.239) | copy-start | bytes 27652
  464.0 321.5 %copy-start.81 = (f32[2,1152]{1,0:T(2,128)}, f32[2,1152]{1,0:T(2,128)S(1)}, u32[]{:S(2)}) copy-start(f32[2,1152]{1,0:T(2,128)S(1)} %get-tuple-element.235) | copy-start | bytes 27652
  555.3 11.7 copy-start.66
  555.3 11.7 copy-start.155
  708.0 11.6 copy-start.5
  708.0 11.6 copy-start.104
  757.2 13.2 copy-start.110
  757.2 13.8 copy-start.88
  757.2 13.8 copy-start.108
  757.2 13.8 copy-start.149
  771.0 14.5 copy-start.10
  771.0 14.5 copy-start.11
  771.0 14.5 copy-start.106
  771.0 14.5 copy-start.147
  785.5 14.2 copy-start.71
  883.5 8.9 copy-start.139
  883.5 8.9 copy-start.1
  883.5 8.9 copy-start.13
  883.5 8.9 copy-start.15
  883.6 8.9 copy-start.114
  899.8 10.3 copy-start.138
  899.8 10.4 copy-start.12
  899.8 10.4 copy-start.14
  899.8 10.4 copy-start.73
  899.8 10.4 copy-start.115
  916.6 10.9 copy-start.17
  931.0 17.3 copy-start.52
  948.3 16.7 copy-start.75
  948.3 16.7 copy-start.126
  948.3 16.7 copy-start.134
  984.2 815.0 %copy-start.154 = (u32[32]{0:T(128)S(1)}, u32[32]{0:T(128)}, u32[]{:S(2)}) copy-start(u32[32]{0:T(128)} %constant.195) | copy-start | bytes 388
  984.2 932.1 %all-gather.18.cloned.1.call-start = ((), (), s32[]{:S(2)}) async-start(), calls=%async_computation.7 | async-start | bytes 8294400 | tf_op jit(solution)/shard_map/all_gather | solution.py:309
  1797.0 3.4 collective-permute-start
  1820.5 232.0 %all-reduce.5.cloned.1.call-start = ((), (), s32[]{:S(2)}) async-start(), calls=%async_computation.8 | async-start | bytes 286720 | tf_op jit(solution)/shard_map/psum | solution.py:318
  1896.0 8.5 copy-start.77
  1896.0 8.5 copy-start.80
  1926.6 8.5 copy-start.4
  (123 other events, 456.9 us)
Sparse Core Ops, SparseCore 0:
  10.2 216.5 all-gather.7
  228.9 117.7 all-gather.9
  348.9 55.0 all-gather.11
  406.0 149.1 all-gather.13
  557.3 150.6 all-gather.15
  984.3 748.6 reduce-scatter.3
  1820.6 57.1 all-gather.17
  1916.3 136.0 all-reduce.4
where the time goes:
time: 2070 us
  waiting for transfers between devices  1140 us (55%)
  local copies, waits for them, and re-layouts  442 us (21%)
  matrix products  327 us (16%)
  other arithmetic  72.9 us (4%)
  blocking collectives  62 us (3%)
    reduce_scatter x1, waiting for transfers between devices, local(): lax.psum_scatter(jnp.concatenate(pieces, axis=1).astype(jnp.bfloat16), 's...  749 us
    gather x2, local copies, waits for them, and re-layouts, local(): jnp.take(relative_table, relative_index(jnp.arange(GRID)), axis=1)  244 us
    all_gather x1, waiting for transfers between devices, local(): lax.all_gather(down_weight, 'seq', axis=0, tiled=True)  132 us
    psum x1, waiting for transfers between devices, local(): lax.psum((heads_part, merge_part, up_part, down_part, modulate_part, tabl...  114 us
    dot_general x9, matrix products, fold_rows(): return jnp.dot(left, portion, preferred_element_type=jnp.float32)  96.1 us
    all_gather x1, waiting for transfers between devices, local(): lax.all_gather(up_weight, 'seq', axis=0, tiled=True)  87.5 us
    dot_general x8, matrix products, right_transposed(): lax.dot_general(left, portion, (((1,), (1,)), ((), ())), preferred_elemen...  77.3 us
    unnamed x359, local copies, waits for them, and re-layouts  65.2 us
  transfers between devices with their start and end apart: 9, of which 6 were waited for; matrix products, arithmetic and copies ran while one was open for 25% of the time, Pallas kernels for 0%

commit v1 on v0

--- a/solution.py
+++ b/solution.py
@@ -1,3 +1,4 @@
+import functools
 from functools import partial
 import math
 import jax
@@ -14,6 +15,24 @@
 SAMP_DEV = 4
 GRID = 256
 epsilon = 1e-06
+
+
+def direct_floor(local_x, a_name):
+    value_now, near = (lax.axis_size(a_name), lax.axis_index(a_name))
+    work_now, tile_out = (local_x, 1)
+    while tile_out < value_now:
+        kept_rows = []
+        for i in range(value_now):
+            kept_rows.append((i, i ^ tile_out))
+        z_new = lax.ppermute(work_now, axis_name=a_name, perm=kept_rows)
+        far_arr = jnp.concatenate([work_now, z_new], axis=0)
+        row_out = jnp.concatenate([z_new, work_now], axis=0)
+        work_now = jnp.where(near & tile_out == 0, far_arr, row_out)
+        tile_out = 2 * tile_out
+    return work_now
+
+
+_post_ranges = functools.partial(direct_floor, a_name="seq")
 
 
 def layer_norm(values):
@@ -219,9 +238,7 @@
         branch = branch.reshape(samples, GRID, D)
         middle = slab + gate_one * branch
         hidden_two = modulated(middle, scale_two, shift_two).astype(jnp.bfloat16).reshape(rows, D)
-        up_value = fold_rows(
-            hidden_two, lax.all_gather(up_weight, "seq", axis=0, tiled=True)
-        ) + up_bias.astype(jnp.float32)
+        up_value = fold_rows(hidden_two, _post_ranges(up_weight)) + up_bias.astype(jnp.float32)
         activated = gelu_tanh(up_value).astype(jnp.bfloat16)
         mlp_out = right_transposed(
             activated, lax.all_gather(down_weight, "seq", axis=0, tiled=True)

time: 2070 us -> 2320 us (1.12)
  waiting for transfers between devices: 1140 us -> 1360 us
    all_gather x1, waiting for transfers between devices: 54.5 us -> 183 us  [local(): lax.all_gather(heads_weight, 'seq', axis=0, tiled=True)]
    all_gather x1, waiting for transfers between devices: 4.54 us -> 87.6 us  [local(): lax.all_gather(merge_weight, 'seq', axis=0, tiled=True)]
    ppermute x0 -> x3, waiting for transfers between devices: none -> 45.3 us  [direct_floor(): z_new = lax.ppermute(work_now, axis_name=a_name, perm=kept_rows)]
    all_gather x1, waiting for transfers between devices: 132 us -> 90.1 us  [local(): lax.all_gather(down_weight, 'seq', axis=0, tiled=True)]
    unnamed x359 -> x419, local copies, waits for them, and re-layouts: 65.2 us -> 62.6 us
  transfers between devices with their start and end apart: 9 -> 12, of which waited for: 6 -> 7; matrix products, arithmetic and copies ran while one was open for 25% -> 24% of each run, Pallas kernels for 0% -> 0%
where the time goes in v1:
time: 2320 us; the launch traced here: 2310 us
  waiting for transfers between devices  1360 us (59%)
  local copies, waits for them, and re-layouts  440 us (19%)
  matrix products  336 us (14%)
  other arithmetic  87.1 us (4%)
  blocking collectives  62 us (3%)
    reduce_scatter x1, waiting for transfers between devices, local(): lax.psum_scatter(jnp.concatenate(pieces, axis=1).astype(jnp.bfloat16), 's...  749 us
    gather x2, local copies, waits for them, and re-layouts, local(): jnp.take(relative_table, relative_index(jnp.arange(GRID)), axis=1)  246 us
    all_gather x1, waiting for transfers between devices, local(): lax.all_gather(heads_weight, 'seq', axis=0, tiled=True)  183 us
    psum x1, waiting for transfers between devices, local(): lax.psum((heads_part, merge_part, up_part, down_part, modulate_part, tabl...  111 us
    dot_general x9, matrix products, fold_rows(): return jnp.dot(left, portion, preferred_element_type=jnp.float32)  101 us
    all_gather x1, waiting for transfers between devices, local(): lax.all_gather(up_weight, 'seq', axis=0, tiled=True)  90.5 us
    all_gather x1, waiting for transfers between devices, local(): lax.all_gather(down_weight, 'seq', axis=0, tiled=True)  90.1 us
    all_gather x1, waiting for transfers between devices, local(): lax.all_gather(merge_weight, 'seq', axis=0, tiled=True)  87.6 us
  transfers between devices with their start and end apart: 12, of which 7 were waited for; matrix products, arithmetic and copies ran while one was open for 24% of the time, Pallas kernels for 0%

profile of v1, /device:TPU:8, one launch (start us, length us, event | category | flops | bytes accessed | tf_op | source)
XLA Modules:
  0.0 2308.6 jit_solution(9363438159363770707)
XLA Ops:
  14.6 45.3 %collective-permute-done = bf16[144,4608]{1,0:T(8,128)(2,1)} collective-permute-done((bf16[144,4608]{1,0:T(8,128)(2,1)}, bf16[144,4608]{1,0:T(8,128)(2,1)}, u32[]{:S(2)}, u32[]{:S(2)}) %collective-permute-start) | collective-permute-done | bytes 1327136 | tf_op jit(solution)/shard_map/ppermute | solution.py:27
  66.5 228.9 %gather_fusion = bf16[65536,16]{1,0:T(8,128)(2,1)} fusion(bf16[16,961]{0,1:T(8,128)(2,1)S(1)} %copy.147, s32[65536]{0:T(1024)S(1)} %broadcast_clamp_fusion), kind=kCustom, calls=%fused_computation | custom fusion | bytes 4456448 | tf_op jit(solution)/shard_map/jit(_take)/gather | solution.py:187
  295.4 16.8 copy.148
  316.5 5.1 convert_bitcast_fusion.1
  330.4 7.7 maximum_select_fusion.1
  340.6 7.8 convolution_add_fusion
  352.5 182.5 %all-gather.10.cloned.1.call-done = bf16[1152,3456]{1,0:T(8,128)(2,1)} async-done(((bf16[144,3456]{1,0:T(8,128)(2,1)}), bf16[1152,3456]{1,0:T(8,128)(2,1)}) %all-gather.10.cloned.1.call-update) | async-done | bytes 7962640 | tf_op jit(solution)/shard_map/all_gather | solution.py:224
  535.0 9.5 add_convert_fusion.1
  544.6 5.8 copy.143
  550.4 8.5 reshape.859
  576.6 87.6 %all-gather.12.cloned.1.call-done = bf16[1152,1152]{1,0:T(8,128)(2,1)} async-done(((bf16[144,1152]{1,0:T(8,128)(2,1)}), bf16[1152,1152]{1,0:T(8,128)(2,1)}) %all-gather.12.cloned.1.call-update) | async-done | bytes 2654224 | tf_op jit(solution)/shard_map/all_gather | solution.py:236
  664.1 7.0 fusion.216
  672.1 10.9 add_convert_fusion
  683.1 5.7 copy.152
  688.8 8.3 reshape.861
  725.3 90.1 %all-gather.14.cloned.1.call-done = bf16[1152,4608]{1,0:T(8,128)(2,1)} async-done(((bf16[144,4608]{1,0:T(8,128)(2,1)}), bf16[1152,4608]{1,0:T(8,128)(2,1)}) %all-gather.14.cloned.1.call-update) | async-done | bytes 10616848 | tf_op jit(solution)/shard_map/all_gather | solution.py:244
  815.4 11.7 fusion.234
  827.1 8.8 fusion.235
  835.9 13.5 fusion.105
  849.3 28.3 %fusion.11 = (bf16[512,4608]{1,0:T(8,128)(2,1)}, bf16[512,4608]{1,0:T(8,128)(2,1)}, bf16[512,4608]{1,0:T(8,128)(2,1)}, bf16[512,4608]{1,0:T(8,128)(2,1)}) fusion(f32[512,4608]{1,0:T(8,128)} %fusion.234, f32[4608]{0:T(1024)} %convert_element_type.243, f32[512,4608]{1,0:T(8,128)} %fusion.105, f32[512,4608]{1,0:T(8,128)} %fusion.235, ...), kind=kOutput, calls=%fused_computation.22 | convolution fusion | flops 5592121344 | bytes 59000832 | tf_op jit(solution)/shard_map/dot_general | solution.py:53
  877.6 90.5 %all-gather.16.cloned.1.call-done = bf16[1152,4608]{1,0:T(8,128)(2,1)} async-done(((bf16[144,4608]{1,0:T(8,128)(2,1)}), bf16[1152,4608]{1,0:T(8,128)(2,1)}) %all-gather.16.cloned.1.call-update) | async-done | bytes 10616848 | tf_op jit(solution)/shard_map/all_gather | solution.py:261
  968.1 13.0 multiply_reduce_fusion.11
  981.7 15.0 fusion.214
  998.0 11.5 multiply_reduce_fusion.9
  1010.1 14.0 fusion.215
  1036.9 5.3 multiply_reduce_fusion.1
  1068.9 5.2 multiply_reduce_fusion
  1087.6 5.5 copy.182
  1097.6 5.4 copy.181
  1103.1 4.8 convolution_convert_fusion.4
  1108.5 10.5 multiply_reduce_fusion.10
  1125.7 10.3 multiply_reduce_fusion.8
  1145.2 5.2 copy.183
  1154.8 14.3 fusion.4
  1171.7 15.7 fusion.3
  1187.4 17.6 fusion.2
  1210.6 4.8 multiply_reduce_fusion.5
  1216.2 8.6 fusion.1
  1224.9 749.0 %reduce-scatter.4.cloned.1.call-done = bf16[144,20736]{1,0:T(8,128)(2,1)} async-done(((bf16[1152,20736]{1,0:T(8,128)(2,1)}), bf16[144,20736]{1,0:T(8,128)(2,1)}) %reduce-scatter.4.cloned.1.call-update) | async-done | bytes 5971984 | tf_op jit(solution)/shard_map/reduce_scatter | solution.py:322
  1973.8 62.0 %fusion = bf16[40,20736]{1,0:T(8,128)(2,1)} fusion(bf16[144,20736]{1,0:T(8,128)(2,1)} %reduce-scatter.4.cloned.1.call-done), kind=kCustom, calls=%all-reduce-scatter | all-reduce-scatter fusion | flops 3317761 | bytes 7631360
  2041.3 17.0 concatenate.102
  2061.6 6.8 fusion.32
  2068.4 8.1 bitcast_add_fusion.2
  2076.5 19.5 add.547
  2096.0 33.3 %fusion.187 = f32[31,16,16,16,1]{0,3,2,4,1:T(8,128)} fusion(f32[16,16,16,16,16]{4,3,2,1,0:T(8,128)} %add.547, s32[16,16]{1,0:T(8,128)S(1)} %subtract_add_fusion), kind=kOutput, calls=%fused_computation.263 | convolution fusion | flops 390078208 | bytes 4703232 | tf_op jit(solution)/shard_map/hwxyz,wya->haxz/dot_general | solution.py:162
  2157.0 10.3 reshape.899
  2167.4 5.3 fusion.220
  2181.9 111.4 %all-reduce.5.cloned.1.call-done = (f32[2304]{0:T(1024)}, f32[1152]{0:T(1024)}, f32[4608]{0:T(1024)}, f32[1152]{0:T(1024)}, f32[6912]{0:T(1024)}, /*index=5*/f32[16,961]{1,0:T(8,128)}) async-done(((f32[2304]{0:T(1024)}, f32[1152]{0:T(1024)}, f32[4608]{0:T(1024)}, f32[1152]{0:T(1024)}, f32[6912]{0:T(1024)}, /*index=5*/f32[16,961]{1,0:T(8,128)}), (f32[2304]{0:T(1024)}, f32[1152]{0:T(1024)}, f32[4608]{0:T(1024)}, ...) | async-done | bytes 126032 | tf_op jit(solution)/shard_map/psum | solution.py:335
  (565 shorter events, 221.8 us)
Async XLA Ops:
  7.2 333.5 %all-gather.8.cloned.1.call-start = ((), (), s32[]{:S(2)}) async-start(), calls=%async_computation.1 | async-start | bytes 17915904 | tf_op jit(solution)/shard_map/all_gather | solution.py:190
  7.9 527.1 %all-gather.10.cloned.1.call-start = ((), (), s32[]{:S(2)}) async-start(), calls=%async_computation.2 | async-start | bytes 8957952 | tf_op jit(solution)/shard_map/all_gather | solution.py:224
  8.7 655.5 %all-gather.12.cloned.1.call-start = ((), (), s32[]{:S(2)}) async-start(), calls=%async_computation.3 | async-start | bytes 2985984 | tf_op jit(solution)/shard_map/all_gather | solution.py:236
  9.4 806.0 %all-gather.14.cloned.1.call-start = ((), (), s32[]{:S(2)}) async-start(), calls=%async_computation.4 | async-start | bytes 11943936 | tf_op jit(solution)/shard_map/all_gather | solution.py:244
  10.0 958.1 %all-gather.16.cloned.1.call-start = ((), (), s32[]{:S(2)}) async-start(), calls=%async_computation.5 | async-start | bytes 11943936 | tf_op jit(solution)/shard_map/all_gather | solution.py:261
  10.0 49.9 %collective-permute-start = (bf16[144,4608]{1,0:T(8,128)(2,1)}, bf16[144,4608]{1,0:T(8,128)(2,1)}, u32[]{:S(2)}, u32[]{:S(2)}) collective-permute-start(bf16[144,4608]{1,0:T(8,128)(2,1)} %param.24), channel_id=1, source_target_pairs={{0,1},{1,0},{2,3},{3,2},{4,5},{5,4},{6,7},{7,6},{8,9},{9,8},{10,11... | collective-permute-start | bytes 3981320 | tf_op jit(solution)/shard_map/ppermute | solution.py:27
  11.6 1962.2 %reduce-scatter.4.cloned.1.call-start = ((), (), s32[]{:S(2)}) async-start(), calls=%async_computation.6 | async-start | bytes 53747712 | tf_op jit(solution)/shard_map/reduce_scatter | solution.py:322
  12.1 53.0 %copy-start.115 = (f32[512]{0:T(512)}, f32[512]{0:T(512)S(1)}, u32[]{:S(2)}) copy-start(f32[512]{0:T(512)S(1)} %get-tuple-element.237) | copy-start | bytes 6148
  12.1 53.5 %copy-start.116 = (f32[512]{0:T(512)}, f32[512]{0:T(512)S(1)}, u32[]{:S(2)}) copy-start(f32[512]{0:T(512)S(1)} %get-tuple-element.236) | copy-start | bytes 6148
  14.5 298.3 %copy-start.150 = (pred[2,256]{1,0:T(4,128)(4,1)}, pred[2,256]{1,0:T(4,128)(4,1)S(1)}, u32[]{:S(2)}) copy-start(pred[2,256]{1,0:T(4,128)(4,1)S(1)} %get-tuple-element.239) | copy-start | bytes 1540
  14.5 298.8 %copy-start.157 = (pred[2,256]{1,0:T(4,128)(4,1)}, pred[2,256]{1,0:T(4,128)(4,1)S(1)}, u32[]{:S(2)}) copy-start(pred[2,256]{1,0:T(4,128)(4,1)S(1)} %get-tuple-element.238) | copy-start | bytes 1540
  14.6 51.7 %copy-start.154 = (bf16[6912]{0:T(1024)(128)(2,1)S(1)}, bf16[6912]{0:T(1024)(128)(2,1)}, u32[]{:S(2)}) copy-start(bf16[6912]{0:T(1024)(128)(2,1)} %param.29) | copy-start | bytes 41476
  14.6 51.7 %copy-start.114 = (bf16[16,961]{1,0:T(8,128)(2,1)S(1)}, bf16[16,961]{1,0:T(8,128)(2,1)}, u32[]{:S(2)}) copy-start(bf16[16,961]{1,0:T(8,128)(2,1)} %param.30) | copy-start | bytes 92260
  63.9 266.5 %collective-permute-start.1 = (bf16[288,4608]{1,0:T(8,128)(2,1)}, bf16[288,4608]{1,0:T(8,128)(2,1)}, u32[]{:S(2)}, u32[]{:S(2)}) collective-permute-start(bf16[288,4608]{1,0:T(8,128)(2,1)} %maximum_select_fusion.2), channel_id=1, source_target_pairs={{0,2},{1,3},{2,0},{3,1},{4,6},{5,7},{6,4},{7,5},{8,10},{9,11},{10,... | collective-permute-start | bytes 7962632 | tf_op jit(solution)/shard_map/ppermute | solution.py:27
  295.4 16.8 copy-start.178
  295.4 18.6 copy-start.156
  295.4 19.2 copy-start.179
  295.4 20.9 copy-start.180
  316.3 247.9 %copy-start.112 = (s32[2,256]{1,0:T(2,128)}, s32[2,256]{1,0:T(2,128)S(1)}, u32[]{:S(2)}) copy-start(s32[2,256]{1,0:T(2,128)S(1)} %get-tuple-element.192) | copy-start | bytes 6148
  338.1 497.7 %collective-permute-start.2 = (bf16[576,4608]{1,0:T(8,128)(2,1)}, bf16[576,4608]{1,0:T(8,128)(2,1)}, u32[]{:S(2)}, u32[]{:S(2)}) collective-permute-start(bf16[576,4608]{1,0:T(8,128)(2,1)} %maximum_select_fusion.1), channel_id=1, source_target_pairs={{0,4},{1,5},{2,6},{3,7},{4,0},{5,1},{6,2},{7,3},{8,12},{9,13},{10,... | collective-permute-start | bytes 15925256 | tf_op jit(solution)/shard_map/ppermute | solution.py:27
  352.5 192.1 %copy-start.67 = (bf16[512,1152]{1,0:T(8,128)(2,1)}, bf16[512,1152]{1,0:T(8,128)(2,1)S(1)}, u32[]{:S(2)}) copy-start(bf16[512,1152]{1,0:T(8,128)(2,1)S(1)} %fusion.98) | copy-start | bytes 3538948
  573.8 90.3 %copy-start.117 = (f32[512]{0:T(512)S(1)}, f32[512]{0:T(512)}, u32[]{:S(2)}) copy-start(f32[512]{0:T(512)} %copy-done.116) | copy-start | bytes 6148
  575.3 95.8 %copy-start.57 = (bf16[144,8,2,256]{3,1,2,0:T(8,128)(2,1)}, bf16[144,8,2,256]{3,1,2,0:T(8,128)(2,1)S(1)}, u32[]{:S(2)}) copy-start(bf16[144,8,2,256]{3,1,2,0:T(8,128)(2,1)S(1)} %copy.251) | copy-start | bytes 3538948
  968.1 13.6 copy-start.9
  968.1 13.6 copy-start.81
  968.1 13.6 copy-start.100
  981.7 16.3 copy-start.11
  981.7 16.3 copy-start.89
  981.7 16.3 copy-start.103
  1009.5 14.7 copy-start.12
  1010.1 14.7 copy-start.77
  1150.5 20.4 slice-start.4
  1154.8 14.3 copy-start.25
  1154.8 16.1 slice-start.5
  1187.3 17.7 copy-start.95
  1187.3 17.7 copy-start.125
  1187.3 17.7 copy-start.16
  1187.3 17.7 copy-start.20
  1187.3 17.7 copy-start.82
  1187.4 17.7 copy-start.137
  1187.4 17.7 copy-start.149
  1187.4 17.7 copy-start.152
  1187.4 17.7 copy-start.161
  1187.4 17.7 copy-start.165
  1224.8 815.2 %copy-start.182 = (u32[32]{0:T(128)S(1)}, u32[32]{0:T(128)}, u32[]{:S(2)}) copy-start(u32[32]{0:T(128)} %constant.198) | copy-start | bytes 388
  1224.8 932.2 %all-gather.18.cloned.1.call-start = ((), (), s32[]{:S(2)}) async-start(), calls=%async_computation.7 | async-start | bytes 8294400 | tf_op jit(solution)/shard_map/all_gather | solution.py:326
  2037.9 3.4 collective-permute-start.3
  2061.4 231.9 %all-reduce.5.cloned.1.call-start = ((), (), s32[]{:S(2)}) async-start(), calls=%async_computation.8 | async-start | bytes 286720 | tf_op jit(solution)/shard_map/psum | solution.py:335
  (155 other events, 730.9 us)
Sparse Core Ops, SparseCore 0:
  10.2 265.4 all-gather.7
  277.9 257.1 all-gather.9
  537.2 126.8 all-gather.11
  666.2 149.1 all-gather.13
  817.4 150.6 all-gather.15
  1224.9 748.8 reduce-scatter.3
  2061.5 57.1 all-gather.17
  2157.1 136.1 all-reduce.4
